TPU v7x, 128 devices: a whole 4x4x4 slice. The times are simulated.
128 devices in a mesh: front: 2 (over core), row: 8 (over y, x_hi), col: 8 (over z, x_lo).
Axes of the slice: x: 4 (x_hi: 2, x_lo: 2; x = x_hi * 2 + x_lo), y: 4, z: 4, core: 2. Of those that a mesh axis runs over, the one named last changes fastest.
Arguments:
- front_matrix: bfloat16 [2, 3, 8, 256, 3, 8, 256], P('front', None, 'row', None, None, 'col'), as said below
- contributions: bfloat16 [2, 8, 8, 32, 256, 256], P('front', 'row', 'col'), may hold values from -3 to 3
- target_front: int32 [2, 8, 8, 32], P('front', 'row', 'col'), may hold values from 0 to 1, as said below
- target_row: int32 [2, 8, 8, 32], P('front', 'row', 'col'), may hold values from 8 to 23, as said below
- target_col: int32 [2, 8, 8, 32], P('front', 'row', 'col'), may hold values from 0 to 22, as said below
- live_count: int32 [2, 8, 8], P('front', 'row', 'col'), may hold values from 24 to 32
Outputs:
- factor: float32 [2, 3, 8, 256, 3, 8, 256], P('front', None, 'row', None, None, 'col')
Inputs may be any that keep to these rules, and one draw needn't show every extreme that they name: `front_matrix`: Symmetric; its leading 2 * 2 * 256 rows and columns form a strictly diagonally dominant block with a positive diagonal. `target_front`: among one device's live slots at most 2 aim at one pair of parent front and target_row modulo the number of row devices, and on every device one such pair takes exactly 2. `target_row`: never one of the first 4 tile rows, nor one of the first tile rows as many as the col devices. `target_col`: below the slot's target_row, and congruent to the holding device's col index modulo the number of col devices.
All inputs are finite; a program needn't handle non-finite values.
Results may differ from a plain program's by a relative error of at most 0.0003.
Values may be sent and summed in bfloat16 or wider, within the bound.
No kernel may reach another device: no remote copies, remote signals or barrier semaphores. Data moves between devices by JAX's collectives and lax.ppermute only.
A program may use at most 128 MiB of HBM per device.

v0:
```python
import jax
import jax.numpy as jnp
import numpy as np
from jax import lax
from jax.sharding import PartitionSpec as P

PANEL_TILES = 2
PANELS = 2


def broadcast(array, axis, root):
    mine = lax.axis_index(axis) == root
    return lax.psum(jnp.where(mine, array, jnp.zeros_like(array)), axis)


def mirror_tiles(square, tile_size):
    tile_ids = jnp.arange(square.shape[0]) // tile_size
    return jnp.where(tile_ids[:, None] >= tile_ids[None, :], square, square.T)


def panel_factor(square, tile_size):
    return jnp.linalg.cholesky(mirror_tiles(square, tile_size))


def below_solve(lead_factor, row_block):
    return lax.linalg.triangular_solve(
        lead_factor, row_block, left_side=False, lower=True, transpose_a=True
    )


def pack_buckets(
    contrib_tiles, destination, live_slots, slot_ids, bucket_total, capacity, local_tile
):
    earlier = (
        (destination[:, None] == destination[None, :])
        & live_slots[None, :]
        & (slot_ids[None, :] < slot_ids[:, None])
    )
    position = jnp.sum(earlier.astype(jnp.int32), axis=1)
    bucket = destination * capacity + position
    matches = (bucket[None, :] == jnp.arange(bucket_total, dtype=jnp.int32)[:, None]) & live_slots[
        None, :
    ]
    source = jnp.sum(jnp.where(matches, slot_ids[None, :], 0), axis=1)
    filled = jnp.any(matches, axis=1)
    packed = jnp.where(filled[:, None, None], contrib_tiles[source], jnp.zeros((), jnp.bfloat16))
    targets = jnp.where(filled, local_tile[source], -1)
    return (packed, targets)


def route_tiles(
    contributions,
    target_front,
    target_row,
    target_col,
    live_count,
    tile_cols,
    n_front,
    n_row,
    n_col,
):
    slot_total = contributions.shape[3]
    tile_size = contributions.shape[4]
    contrib_tiles = contributions.reshape(slot_total, tile_size, tile_size)
    fronts_to = target_front.reshape(slot_total)
    rows_to = target_row.reshape(slot_total)
    cols_to = target_col.reshape(slot_total)
    slot_ids = jnp.arange(slot_total, dtype=jnp.int32)
    live_slots = slot_ids < live_count.reshape(())
    capacity = max(2, -(-slot_total // (n_front * n_row)))
    local_tile = rows_to // n_row * tile_cols + cols_to // n_col
    destination = fronts_to * n_row + rows_to % n_row
    bucket_total = n_front * n_row * capacity
    packed, targets = pack_buckets(
        contrib_tiles, destination, live_slots, slot_ids, bucket_total, capacity, local_tile
    )
    received, arrived = (
        lax.all_to_all(packed, ("front", "row"), split_axis=0, concat_axis=0, tiled=True),
        lax.all_to_all(targets, ("front", "row"), split_axis=0, concat_axis=0, tiled=True),
    )
    return (received, arrived)


def per_device(front_matrix, contributions, target_front, target_row, target_col, live_count):
    tile_rows = front_matrix.shape[1]
    tile_size = front_matrix.shape[3]
    tile_cols = front_matrix.shape[4]
    n_front = lax.axis_size("front")
    n_row = lax.axis_size("row")
    n_col = lax.axis_size("col")
    row_index = lax.axis_index("row")
    col_index = lax.axis_index("col")
    work = front_matrix.reshape(tile_rows, tile_size, tile_cols, tile_size).astype(jnp.float32)
    received, arrived = route_tiles(
        contributions,
        target_front,
        target_row,
        target_col,
        live_count,
        tile_cols,
        n_front,
        n_row,
        n_col,
    )
    local_total = tile_rows * tile_cols
    selector = (arrived[None, :] == jnp.arange(local_total, dtype=jnp.int32)[:, None]).astype(
        jnp.bfloat16
    )
    assembled = jnp.dot(
        selector,
        received.reshape(received.shape[0], tile_size * tile_size),
        preferred_element_type=jnp.float32,
    )
    work = work + assembled.reshape(tile_rows, tile_cols, tile_size, tile_size).transpose(
        0, 2, 1, 3
    )
    global_rows = jnp.arange(tile_rows, dtype=jnp.int32) * n_row + row_index
    global_cols = jnp.arange(tile_cols, dtype=jnp.int32) * n_col + col_index
    panel_width = PANEL_TILES * tile_size
    for panel_number in range(PANELS):
        first_tile = panel_number * PANEL_TILES
        after_tile = first_tile + PANEL_TILES
        pieces = []
        for member in range(PANEL_TILES):
            tile_index = first_tile + member
            pieces.append(broadcast(work[:, :, tile_index // n_col, :], "col", tile_index % n_col))
        rows_panel = jnp.concatenate(pieces, axis=2)
        diagonal_part = jnp.stack(
            [
                jnp.where(
                    row_index == (first_tile + member) % n_row,
                    rows_panel[(first_tile + member) // n_row],
                    0.0,
                )
                for member in range(PANEL_TILES)
            ]
        )
        lead_block = (
            lax.psum(diagonal_part.astype(jnp.bfloat16), "row")
            .astype(jnp.float32)
            .reshape(panel_width, panel_width)
        )
        lead_factor = panel_factor(lead_block, tile_size)
        solved = below_solve(
            lead_factor, rows_panel.reshape(tile_rows * tile_size, panel_width)
        ).reshape(tile_rows, tile_size, panel_width)
        offset = global_rows - first_tile
        in_panel = (offset >= 0) & (offset < PANEL_TILES)
        picked = lead_factor.reshape(PANEL_TILES, tile_size, panel_width)[
            jnp.clip(offset, 0, PANEL_TILES - 1)
        ]
        row_mask = global_rows >= after_tile
        factor_rows = jnp.where(
            row_mask[:, None, None], solved, jnp.where(in_panel[:, None, None], picked, 0.0)
        )
        grouped = factor_rows.reshape(tile_cols, n_col // n_row, tile_size, panel_width)
        own_piece = lax.dynamic_index_in_dim(grouped, col_index // n_row, axis=1, keepdims=False)
        cols_panel = broadcast(own_piece, "row", col_index % n_row)
        col_mask = global_cols >= after_tile
        for member in range(PANEL_TILES):
            tile_index = first_tile + member
            local_col = tile_index // n_col
            owner = col_index == tile_index % n_col
            stored = jnp.where(
                owner,
                factor_rows[:, :, member * tile_size : (member + 1) * tile_size],
                work[:, :, local_col, :],
            )
            work = work.at[:, :, local_col, :].set(stored)
        early_slots = []
        late_slots = [
            slot_number for slot_number in range(tile_cols) if slot_number not in early_slots
        ]
        for group_slots in (early_slots, late_slots):
            if group_slots:
                indices = np.array(group_slots, dtype=np.int32)
                update = jnp.einsum(
                    "atk,bsk->atbs",
                    factor_rows,
                    cols_panel[indices],
                    precision=lax.Precision.HIGHEST,
                    preferred_element_type=jnp.float32,
                )
                trailing_mask = (
                    row_mask[:, None, None, None] & col_mask[indices][None, None, :, None]
                )
                work = work.at[:, :, indices, :].add(-jnp.where(trailing_mask, update, 0.0))
    lower = global_rows[:, None] >= global_cols[None, :]
    factor = jnp.where(lower[:, None, :, None], work, 0.0)
    return factor.reshape(1, tile_rows, 1, tile_size, tile_cols, 1, tile_size)


def solution(mesh):
    in_specs = (
        P("front", None, "row", None, None, "col", None),
        P("front", "row", "col", None, None, None),
        P("front", "row", "col", None),
        P("front", "row", "col", None),
        P("front", "row", "col", None),
        P("front", "row", "col"),
    )
    out_specs = P("front", None, "row", None, None, "col", None)
    return jax.shard_map(
        per_device, mesh=mesh, in_specs=in_specs, out_specs=out_specs, check_vma=False
    )
```

profile of v0, /device:TPU:0, one launch (start us, length us, event | category | flops | bytes accessed | tf_op | source)
XLA Modules:
  0.0 1018.7 jit_solution(2382640748277828764)
XLA Ops:
  9.8 7.1 all-to-all-start
  26.4 7.4 all-to-all-start.1
  35.1 50.3 %all-to-all-done.1 = bf16[32,256,256]{2,1,0:T(8,128)(2,1)} async-done(((bf16[32,256,256]{2,1,0:T(8,128)(2,1)}), bf16[32,256,256]{2,1,0:T(8,128)(2,1)}, u32[]{:S(2)}, u32[]{:S(2)}) %all-to-all-start.1) | async-done | bytes 4194336 | tf_op jit(solution)/shard_map/all_to_all | solution.py:78
  85.5 5.6 convert_add_fusion
  93.4 86.9 %all-reduce.20.cloned.1.call-done = (f32[3,256,256]{2,1,0:T(8,128)}, f32[3,256,256]{2,1,0:T(8,128)}) async-done(((f32[3,256,256]{2,1,0:T(8,128)}, f32[3,256,256]{2,1,0:T(8,128)}), (f32[3,256,256]{2,1,0:T(8,128)}, f32[3,256,256]{2,1,0:T(8,128)})) %all-reduce.20.cloned.1.call-update) | async-done | bytes 1572880 | tf_op jit(solution)/shard_map/psum | solution.py:13
  185.3 84.4 %all-reduce.10.cloned.1.call-done = bf16[512,512]{1,0:T(8,128)(2,1)} async-done(((bf16[512,512]{1,0:T(8,128)(2,1)}), bf16[512,512]{1,0:T(8,128)(2,1)}) %all-reduce.10.cloned.1.call-update) | async-done | bytes 524304 | tf_op jit(solution)/shard_map/psum | solution.py:139
  273.7 11.7 %cholesky.286 = f32[128,128]{1,0:T(8,128)S(1)} custom-call(f32[128,128]{1,0:T(8,128)S(1)} %cholesky.426), custom_call_target="Cholesky" | custom-call | tf_op jit(solution)/shard_map/jit(cholesky)/cholesky | solution.py:22
  285.6 9.8 custom-call.27
  298.0 11.7 %cholesky.305 = f32[128,128]{1,0:T(8,128)S(1)} custom-call(f32[128,128]{1,0:T(8,128)S(1)} %cholesky.430), custom_call_target="Cholesky" | custom-call | tf_op jit(solution)/shard_map/jit(cholesky)/cholesky | solution.py:22
  309.7 10.2 %custom-call.28 = f32[1,128,128]{1,2,0:T(8,128)S(1)} custom-call(f32[1,128,128]{2,1,0:T(8,128)S(1)} %get-tuple-element.129), custom_call_target="InvertDiagBlocksLowerTriangular" | custom-call | tf_op jit(solution)/shard_map/jit(cholesky)/cholesky | solution.py:22
  321.5 11.7 %cholesky.326 = f32[128,128]{1,0:T(8,128)S(1)} custom-call(f32[128,128]{1,0:T(8,128)S(1)} %cholesky.435), custom_call_target="Cholesky" | custom-call | tf_op jit(solution)/shard_map/jit(cholesky)/cholesky | solution.py:22
  333.9 9.8 custom-call.29
  345.2 11.8 %cholesky.343 = f32[128,128]{1,0:T(8,128)S(1)} custom-call(f32[128,128]{1,0:T(8,128)S(1)} %convolution_subtract_fusion.11), custom_call_target="Cholesky" | custom-call | tf_op jit(solution)/shard_map/jit(cholesky)/cholesky | solution.py:22
  362.4 12.2 %while.8 = (s32[]{:T(128)}, f32[512,512]{1,0:T(8,128)}, s32[4,2]{0,1:T(2,128)S(1)}, f32[4,128,128]{2,1,0:T(8,128)S(1)}, s32[]{:T(128)}) while((s32[]{:T(128)}, f32[512,512]{1,0:T(8,128)}, s32[4,2]{0,1:T(2,128)S(1)}, f32[4,128,128]{2,1,0:T(8,128)S(1)}, s32[]{:T(128)}) %tuple.82), condition=%wide.while_cond.4, body=%wide.while_body.4.sunk | while | flops 2 | bytes 131181 | solution.py:26
  374.7 39.3 %custom-call.30 = f32[4,128,128]{1,2,0:T(8,128)S(1)} custom-call(f32[4,128,128]{2,1,0:T(8,128)S(1)} %get-tuple-element.69), custom_call_target="InvertDiagBlocksLowerTriangular" | custom-call | tf_op jit(solution)/shard_map/triangular_solve/custom-call.3 | solution.py:26
  437.1 17.9 %scatter.14 = f32[3,256,3,256]{3,2,1,0:T(4,128)} dynamic-update-slice(f32[3,256,3,256]{3,2,1,0:T(4,128)} %copy-done.3, f32[3,256,1,256]{3,2,1,0:T(1,128)S(1)} %copy.73, s32[]{:T(128)} %copy.158, s32[]{:T(128)} %copy.158, s32[]{:T(128)} %copy.158, s32[]{:T(128)} %copy.158) | dynamic-update-slice | bytes 1572868 | tf_op jit(solution)/shard_map/scatter | solution.py:169
  455.5 17.9 %scatter.15 = f32[3,256,3,256]{3,2,1,0:T(4,128)} dynamic-update-slice(f32[3,256,3,256]{3,2,1,0:T(4,128)} %scatter.14, f32[3,256,1,256]{3,2,1,0:T(1,128)S(1)} %reshape.562, s32[]{:T(128)} %copy.158, s32[]{:T(128)} %copy.158, s32[]{:T(128)} %copy.158, s32[]{:T(128)} %copy.158) | dynamic-update-slice | bytes 1572868 | tf_op jit(solution)/shard_map/scatter | solution.py:169
  475.8 52.9 %all-reduce.12.cloned.1.call-done = f32[3,256,512]{2,1,0:T(8,128)} async-done(((f32[3,256,512]{2,1,0:T(8,128)}), f32[3,256,512]{2,1,0:T(8,128)}) %all-reduce.12.cloned.1.call-update) | async-done | bytes 1572880 | tf_op jit(solution)/shard_map/psum | solution.py:13
  531.8 6.0 negate_bitcast_fusion.1
  545.0 85.8 %all-reduce.18.cloned.1.call-done = (f32[3,256,256]{2,1,0:T(8,128)}, f32[3,256,256]{2,1,0:T(8,128)}) async-done(((f32[3,256,256]{2,1,0:T(8,128)}, f32[3,256,256]{2,1,0:T(8,128)}), (f32[3,256,256]{2,1,0:T(8,128)}, f32[3,256,256]{2,1,0:T(8,128)})) %all-reduce.18.cloned.1.call-update) | async-done | bytes 1572880 | tf_op jit(solution)/shard_map/psum | solution.py:13
  634.8 85.3 %all-reduce.14.cloned.1.call-done = bf16[512,512]{1,0:T(8,128)(2,1)} async-done(((bf16[512,512]{1,0:T(8,128)(2,1)}), bf16[512,512]{1,0:T(8,128)(2,1)}) %all-reduce.14.cloned.1.call-update) | async-done | bytes 524304 | tf_op jit(solution)/shard_map/psum | solution.py:139
  727.7 11.7 %cholesky.358 = f32[128,128]{1,0:T(8,128)S(1)} custom-call(f32[128,128]{1,0:T(8,128)S(1)} %cholesky.439), custom_call_target="Cholesky" | custom-call | tf_op jit(solution)/shard_map/jit(cholesky)/cholesky | solution.py:22
  740.2 9.8 custom-call.31
  753.2 11.7 %cholesky.377 = f32[128,128]{1,0:T(8,128)S(1)} custom-call(f32[128,128]{1,0:T(8,128)S(1)} %cholesky.443), custom_call_target="Cholesky" | custom-call | tf_op jit(solution)/shard_map/jit(cholesky)/cholesky | solution.py:22
  767.0 9.9 custom-call.32
  780.0 13.2 %cholesky.398 = f32[128,128]{1,0:T(8,128)} custom-call(f32[128,128]{1,0:T(8,128)} %cholesky.448), custom_call_target="Cholesky" | custom-call | tf_op jit(solution)/shard_map/jit(cholesky)/cholesky | solution.py:22
  795.4 11.3 %custom-call.33 = f32[1,128,128]{1,2,0:T(8,128)} custom-call(f32[1,128,128]{2,1,0:T(8,128)} %get-tuple-element.116), custom_call_target="InvertDiagBlocksLowerTriangular" | custom-call | tf_op jit(solution)/shard_map/jit(cholesky)/cholesky | solution.py:22
  808.9 11.9 %cholesky.415 = f32[128,128]{1,0:T(8,128)S(1)} custom-call(f32[128,128]{1,0:T(8,128)S(1)} %convolution_subtract_fusion.10), custom_call_target="Cholesky" | custom-call | tf_op jit(solution)/shard_map/jit(cholesky)/cholesky | solution.py:22
  825.8 11.7 %while.9 = (s32[]{:T(128)}, f32[512,512]{1,0:T(8,128)}, s32[4,2]{0,1:T(2,128)S(1)}, f32[4,128,128]{2,1,0:T(8,128)S(1)}, s32[]{:T(128)}) while((s32[]{:T(128)}, f32[512,512]{1,0:T(8,128)}, s32[4,2]{0,1:T(2,128)S(1)}, f32[4,128,128]{2,1,0:T(8,128)S(1)}, s32[]{:T(128)}) %tuple.102), condition=%wide.while_cond.4.clone, body=%wide.while_body.4.clone.sunk | while | flops 2 | bytes 131181 | solution.py:26
  837.5 39.3 %custom-call.34 = f32[4,128,128]{1,2,0:T(8,128)S(1)} custom-call(f32[4,128,128]{2,1,0:T(8,128)S(1)} %get-tuple-element.70), custom_call_target="InvertDiagBlocksLowerTriangular" | custom-call | tf_op jit(solution)/shard_map/triangular_solve/custom-call.3 | solution.py:26
  900.3 91.7 %all-reduce.16.cloned.1.call-done = f32[3,256,512]{2,1,0:T(8,128)} async-done(((f32[3,256,512]{2,1,0:T(8,128)}), f32[3,256,512]{2,1,0:T(8,128)}) %all-reduce.16.cloned.1.call-update) | async-done | bytes 1572880 | tf_op jit(solution)/shard_map/psum | solution.py:13
  995.2 6.0 negate_bitcast_fusion
  (200 shorter events, 157.8 us)
Async XLA Ops:
  9.8 16.6 %all-to-all-start = ((s32[16,2,1]{1,2,0:T(1,128)}), s32[16,2,1]{1,2,0:T(1,128)S(1)}, u32[]{:S(2)}, u32[]{:S(2)}) async-start(s32[16,2,1]{1,2,0:T(1,128)} %bitcast.7), calls=%async_computation | async-start | bytes 16384 | tf_op jit(solution)/shard_map/all_to_all | solution.py:79
  26.4 59.1 %copy-start.15 = (bf16[1,3,1,256,3,1,256]{6,3,5,4,2,1,0:T(8,128)(2,1)S(1)}, bf16[1,3,1,256,3,1,256]{6,3,5,4,2,1,0:T(8,128)(2,1)}, u32[]{:S(2)}) copy-start(bf16[1,3,1,256,3,1,256]{6,3,5,4,2,1,0:T(8,128)(2,1)} %param.25) | copy-start | bytes 3538948
  26.4 59.1 %all-to-all-start.1 = ((bf16[32,256,256]{2,1,0:T(8,128)(2,1)}), bf16[32,256,256]{2,1,0:T(8,128)(2,1)}, u32[]{:S(2)}, u32[]{:S(2)}) async-start(bf16[32,256,256]{2,1,0:T(8,128)(2,1)} %broadcast_select_fusion), calls=%async_computation.1 | async-start | bytes 8388608 | tf_op jit(solution)/shard_map/all_to_all | solution.py:78
  33.8 146.5 %all-reduce.20.cloned.1.call-start = ((), (), s32[]{:S(2)}) async-start(), calls=%async_computation.7 | async-start | bytes 3145728 | tf_op jit(solution)/shard_map/psum | solution.py:13
  91.1 2.2 copy-start.3
  93.3 176.4 %all-reduce.10.cloned.1.call-start = ((), (), s32[]{:S(2)}) async-start(), calls=%async_computation.2 | async-start | bytes 1048576 | tf_op jit(solution)/shard_map/psum | solution.py:139
  180.3 1.4 copy-start.10
  181.8 1.2 copy-start.4
  183.9 344.7 %all-reduce.12.cloned.1.call-start = ((), (), s32[]{:S(2)}) async-start(), calls=%async_computation.3 | async-start | bytes 3145728 | tf_op jit(solution)/shard_map/psum | solution.py:13
  272.7 1.0 copy-start.9
  434.2 2.1 copy-start.1
  434.2 196.5 %all-reduce.18.cloned.1.call-start = ((), (), s32[]{:S(2)}) async-start(), calls=%async_computation.6 | async-start | bytes 3145728 | tf_op jit(solution)/shard_map/psum | solution.py:13
  436.3 18.7 %copy-start.7 = (f32[3,256,256]{2,1,0:T(8,128)S(1)}, f32[3,256,256]{2,1,0:T(8,128)}, u32[]{:S(2)}) copy-start(f32[3,256,256]{2,1,0:T(8,128)} %get-tuple-element.105) | copy-start | bytes 2359300
  544.9 175.2 %all-reduce.14.cloned.1.call-start = ((), (), s32[]{:S(2)}) async-start(), calls=%async_computation.4 | async-start | bytes 1048576 | tf_op jit(solution)/shard_map/psum | solution.py:139
  630.8 1.4 copy-start.11
  632.2 1.2 copy-start.5
  634.3 357.7 %all-reduce.16.cloned.1.call-start = ((), (), s32[]{:S(2)}) async-start(), calls=%async_computation.5 | async-start | bytes 3145728 | tf_op jit(solution)/shard_map/psum | solution.py:13
  726.7 1.0 copy-start.8
  752.5 0.7 copy-start.12
  876.9 4.0 copy-start.6
  888.6 3.1 copy-start.2
  891.7 1.8 copy-start.13
  891.7 1.8 copy-start.14
  898.6 1.6 copy-start
Sparse Core Ops, SparseCore 0:
  93.5 86.7 all-reduce.19
  184.0 85.6 all-reduce.9
  434.4 94.2 all-reduce.11
  545.1 85.6 all-reduce.17
  634.4 85.6 all-reduce.13
  897.9 94.0 all-reduce.15
where the time goes:
time: 1030 us; the launch traced here: 1020 us
  waiting for transfers between devices  537 us (52%)
  other arithmetic  284 us (28%)
  local copies, waits for them, and re-layouts  109 us (11%)
  matrix products  51.3 us (5%)
  between operations  20.6 us (2%)
  starting transfers between devices  15.6 us (2%)
    psum x4, waiting for transfers between devices, broadcast(): return lax.psum(jnp.where(mine, array, jnp.zeros_like(array)), axis)  317 us
    psum x2, waiting for transfers between devices, per_device(): lax.psum(diagonal_part.astype(jnp.bfloat16), 'row').astype(jnp.float32)  170 us
    another operation x29, other arithmetic, panel_factor(): return jnp.linalg.cholesky(mirror_tiles(square, tile_size))  164 us
    another operation x7, other arithmetic, below_solve(): lax.linalg.triangular_solve(lead_factor, row_block, left_side=False, lowe...  84 us
    all_to_all x1, waiting for transfers between devices, route_tiles(): lax.all_to_all(packed, ('front', 'row'), split_axis=0, concat_axis=0, til...  50.3 us
    scatter x4, local copies, waits for them, and re-layouts, per_device(): work = work.at[:, :, local_col, :].set(stored)  38.1 us
    another operation x29, local copies, waits for them, and re-layouts, below_solve(): lax.linalg.triangular_solve(lead_factor, row_block, left_side=False, lowe...  30 us
    another operation x14, matrix products, below_solve(): lax.linalg.triangular_solve(lead_factor, row_block, left_side=False, lowe...  21 us
  transfers between devices with their start and end apart: 8, of which 7 were waited for; matrix products, arithmetic and copies ran while one was open for 5% of the time, Pallas kernels for 0%

commit v1 on v0

--- a/solution.py
+++ b/solution.py
@@ -136,7 +136,7 @@
             ]
         )
         lead_block = (
-            lax.psum(diagonal_part.astype(jnp.bfloat16), "row")
+            jnp.sum(lax.all_gather(diagonal_part.astype(jnp.bfloat16), "row"), axis=0)
             .astype(jnp.float32)
             .reshape(panel_width, panel_width)
         )

time: 1030 us -> 1000 us (0.971)
  waiting for transfers between devices: 537 us -> 507 us
    psum x2 -> x0, waiting for transfers between devices: 170 us -> none  [per_device(): lax.psum(diagonal_part.astype(jnp.bfloat16), 'row').astype(jnp.float32)]
    all_gather x0 -> x2, waiting for transfers between devices: none -> 139 us  [per_device(): lax.all_gather(diagonal_part.astype(jnp.bfloat16), 'row')]
  transfers between devices with their start and end apart: 8 -> 8, of which waited for: 7 -> 7; matrix products, arithmetic and copies ran while one was open for 5% -> 6% of each run, Pallas kernels for 0% -> 0%
where the time goes in v1:
time: 1000 us; the launch traced here: 996 us
  waiting for transfers between devices  507 us (51%)
  other arithmetic  292 us (29%)
  local copies, waits for them, and re-layouts  110 us (11%)
  matrix products  51.3 us (5%)
  between operations  20.5 us (2%)
  starting transfers between devices  15.6 us (2%)
    psum x4, waiting for transfers between devices, broadcast(): return lax.psum(jnp.where(mine, array, jnp.zeros_like(array)), axis)  318 us
    another operation x29, other arithmetic, panel_factor(): return jnp.linalg.cholesky(mirror_tiles(square, tile_size))  164 us
    all_gather x2, waiting for transfers between devices, per_device(): lax.all_gather(diagonal_part.astype(jnp.bfloat16), 'row')  139 us
    another operation x7, other arithmetic, below_solve(): lax.linalg.triangular_solve(lead_factor, row_block, left_side=False, lowe...  84 us
    all_to_all x1, waiting for transfers between devices, route_tiles(): lax.all_to_all(packed, ('front', 'row'), split_axis=0, concat_axis=0, til...  50.3 us
    scatter x4, local copies, waits for them, and re-layouts, per_device(): work = work.at[:, :, local_col, :].set(stored)  38.2 us
    another operation x29, local copies, waits for them, and re-layouts, below_solve(): lax.linalg.triangular_solve(lead_factor, row_block, left_side=False, lowe...  29.7 us
    another operation x14, matrix products, below_solve(): lax.linalg.triangular_solve(lead_factor, row_block, left_side=False, lowe...  21 us
  transfers between devices with their start and end apart: 8, of which 7 were waited for; matrix products, arithmetic and copies ran while one was open for 6% of the time, Pallas kernels for 0%

profile of v1, /device:TPU:0, one launch (start us, length us, event | category | flops | bytes accessed | tf_op | source)
XLA Modules:
  0.0 995.7 jit_solution(1705452740004625596)
XLA Ops:
  9.8 7.1 all-to-all-start
  26.4 7.4 all-to-all-start.1
  35.1 50.3 %all-to-all-done.1 = bf16[32,256,256]{2,1,0:T(8,128)(2,1)} async-done(((bf16[32,256,256]{2,1,0:T(8,128)(2,1)}), bf16[32,256,256]{2,1,0:T(8,128)(2,1)}, u32[]{:S(2)}, u32[]{:S(2)}) %all-to-all-start.1) | async-done | bytes 4194336 | tf_op jit(solution)/shard_map/all_to_all | solution.py:78
  85.5 5.6 convert_add_fusion
  93.4 86.9 %all-reduce.14.cloned.1.call-done = (f32[3,256,256]{2,1,0:T(8,128)}, f32[3,256,256]{2,1,0:T(8,128)}) async-done(((f32[3,256,256]{2,1,0:T(8,128)}, f32[3,256,256]{2,1,0:T(8,128)}), (f32[3,256,256]{2,1,0:T(8,128)}, f32[3,256,256]{2,1,0:T(8,128)})) %all-reduce.14.cloned.1.call-update) | async-done | bytes 1572880 | tf_op jit(solution)/shard_map/psum | solution.py:13
  185.3 68.9 %all-gather.3.cloned.1.call-done = bf16[8,2,256,512]{3,2,1,0:T(8,128)(2,1)} async-done(((bf16[1,2,256,512]{3,2,1,0:T(8,128)(2,1)}), bf16[8,2,256,512]{3,2,1,0:T(8,128)(2,1)}) %all-gather.3.cloned.1.call-update) | async-done | bytes 4194320 | tf_op jit(solution)/shard_map/all_gather | solution.py:139
  261.6 11.7 %cholesky.286 = f32[128,128]{1,0:T(8,128)S(1)} custom-call(f32[128,128]{1,0:T(8,128)S(1)} %cholesky.426), custom_call_target="Cholesky" | custom-call | tf_op jit(solution)/shard_map/jit(cholesky)/cholesky | solution.py:22
  273.5 9.8 custom-call.27
  285.9 12.1 %cholesky.305 = f32[128,128]{1,0:T(8,128)S(1)} custom-call(f32[128,128]{1,0:T(8,128)S(1)} %cholesky.430), custom_call_target="Cholesky" | custom-call | tf_op jit(solution)/shard_map/jit(cholesky)/cholesky | solution.py:22
  298.0 9.8 custom-call.28
  309.4 11.7 %cholesky.326 = f32[128,128]{1,0:T(8,128)S(1)} custom-call(f32[128,128]{1,0:T(8,128)S(1)} %cholesky.435), custom_call_target="Cholesky" | custom-call | tf_op jit(solution)/shard_map/jit(cholesky)/cholesky | solution.py:22
  321.8 9.8 custom-call.29
  333.1 11.9 %cholesky.343 = f32[128,128]{1,0:T(8,128)S(1)} custom-call(f32[128,128]{1,0:T(8,128)S(1)} %convolution_subtract_fusion.11), custom_call_target="Cholesky" | custom-call | tf_op jit(solution)/shard_map/jit(cholesky)/cholesky | solution.py:22
  350.4 12.2 %while.8 = (s32[]{:T(128)}, f32[512,512]{1,0:T(8,128)}, s32[4,2]{0,1:T(2,128)S(1)}, f32[4,128,128]{2,1,0:T(8,128)S(1)}, s32[]{:T(128)}) while((s32[]{:T(128)}, f32[512,512]{1,0:T(8,128)}, s32[4,2]{0,1:T(2,128)S(1)}, f32[4,128,128]{2,1,0:T(8,128)S(1)}, s32[]{:T(128)}) %tuple.82), condition=%wide.while_cond.4, body=%wide.while_body.4.sunk | while | flops 2 | bytes 131181 | solution.py:26
  362.6 39.3 %custom-call.30 = f32[4,128,128]{1,2,0:T(8,128)S(1)} custom-call(f32[4,128,128]{2,1,0:T(8,128)S(1)} %get-tuple-element.69), custom_call_target="InvertDiagBlocksLowerTriangular" | custom-call | tf_op jit(solution)/shard_map/triangular_solve/custom-call.3 | solution.py:26
  425.0 17.9 %scatter.14 = f32[3,256,3,256]{3,2,1,0:T(4,128)} dynamic-update-slice(f32[3,256,3,256]{3,2,1,0:T(4,128)} %copy-done.3, f32[3,256,1,256]{3,2,1,0:T(1,128)S(1)} %copy.73, s32[]{:T(128)} %copy.156, s32[]{:T(128)} %copy.156, s32[]{:T(128)} %copy.156, s32[]{:T(128)} %copy.156) | dynamic-update-slice | bytes 1572868 | tf_op jit(solution)/shard_map/scatter | solution.py:169
  443.5 17.9 %scatter.15 = f32[3,256,3,256]{3,2,1,0:T(4,128)} dynamic-update-slice(f32[3,256,3,256]{3,2,1,0:T(4,128)} %scatter.14, f32[3,256,1,256]{3,2,1,0:T(1,128)S(1)} %reshape.618, s32[]{:T(128)} %copy.156, s32[]{:T(128)} %copy.156, s32[]{:T(128)} %copy.156, s32[]{:T(128)} %copy.156) | dynamic-update-slice | bytes 1572868 | tf_op jit(solution)/shard_map/scatter | solution.py:169
  463.7 53.0 %all-reduce.8.cloned.1.call-done = f32[3,256,512]{2,1,0:T(8,128)} async-done(((f32[3,256,512]{2,1,0:T(8,128)}), f32[3,256,512]{2,1,0:T(8,128)}) %all-reduce.8.cloned.1.call-update) | async-done | bytes 1572880 | tf_op jit(solution)/shard_map/psum | solution.py:13
  519.9 6.0 negate_bitcast_fusion.1
  533.1 85.8 %all-reduce.12.cloned.1.call-done = (f32[3,256,256]{2,1,0:T(8,128)}, f32[3,256,256]{2,1,0:T(8,128)}) async-done(((f32[3,256,256]{2,1,0:T(8,128)}, f32[3,256,256]{2,1,0:T(8,128)}), (f32[3,256,256]{2,1,0:T(8,128)}, f32[3,256,256]{2,1,0:T(8,128)})) %all-reduce.12.cloned.1.call-update) | async-done | bytes 1572880 | tf_op jit(solution)/shard_map/psum | solution.py:13
  623.0 69.9 %all-gather.5.cloned.1.call-done = bf16[8,2,256,512]{3,2,1,0:T(8,128)(2,1)} async-done(((bf16[1,2,256,512]{3,2,1,0:T(8,128)(2,1)}), bf16[8,2,256,512]{3,2,1,0:T(8,128)(2,1)}) %all-gather.5.cloned.1.call-update) | async-done | bytes 4194320 | tf_op jit(solution)/shard_map/all_gather | solution.py:139
  704.9 11.7 %cholesky.358 = f32[128,128]{1,0:T(8,128)S(1)} custom-call(f32[128,128]{1,0:T(8,128)S(1)} %cholesky.439), custom_call_target="Cholesky" | custom-call | tf_op jit(solution)/shard_map/jit(cholesky)/cholesky | solution.py:22
  717.4 9.8 custom-call.31
  730.4 11.8 %cholesky.377 = f32[128,128]{1,0:T(8,128)S(1)} custom-call(f32[128,128]{1,0:T(8,128)S(1)} %cholesky.443), custom_call_target="Cholesky" | custom-call | tf_op jit(solution)/shard_map/jit(cholesky)/cholesky | solution.py:22
  744.3 9.8 custom-call.32
  757.1 13.2 %cholesky.398 = f32[128,128]{1,0:T(8,128)} custom-call(f32[128,128]{1,0:T(8,128)} %cholesky.448), custom_call_target="Cholesky" | custom-call | tf_op jit(solution)/shard_map/jit(cholesky)/cholesky | solution.py:22
  772.5 11.3 %custom-call.33 = f32[1,128,128]{1,2,0:T(8,128)} custom-call(f32[1,128,128]{2,1,0:T(8,128)} %get-tuple-element.116), custom_call_target="InvertDiagBlocksLowerTriangular" | custom-call | tf_op jit(solution)/shard_map/jit(cholesky)/cholesky | solution.py:22
  786.0 11.9 %cholesky.415 = f32[128,128]{1,0:T(8,128)S(1)} custom-call(f32[128,128]{1,0:T(8,128)S(1)} %convolution_subtract_fusion.10), custom_call_target="Cholesky" | custom-call | tf_op jit(solution)/shard_map/jit(cholesky)/cholesky | solution.py:22
  802.8 11.5 %while.9 = (s32[]{:T(128)}, f32[512,512]{1,0:T(8,128)}, s32[4,2]{0,1:T(2,128)S(1)}, f32[4,128,128]{2,1,0:T(8,128)S(1)}, s32[]{:T(128)}) while((s32[]{:T(128)}, f32[512,512]{1,0:T(8,128)}, s32[4,2]{0,1:T(2,128)S(1)}, f32[4,128,128]{2,1,0:T(8,128)S(1)}, s32[]{:T(128)}) %tuple.102), condition=%wide.while_cond.4.clone, body=%wide.while_body.4.clone.sunk | while | flops 2 | bytes 131181 | solution.py:26
  814.4 39.3 %custom-call.34 = f32[4,128,128]{1,2,0:T(8,128)S(1)} custom-call(f32[4,128,128]{2,1,0:T(8,128)S(1)} %get-tuple-element.70), custom_call_target="InvertDiagBlocksLowerTriangular" | custom-call | tf_op jit(solution)/shard_map/triangular_solve/custom-call.3 | solution.py:26
  877.2 91.9 %all-reduce.10.cloned.1.call-done = f32[3,256,512]{2,1,0:T(8,128)} async-done(((f32[3,256,512]{2,1,0:T(8,128)}), f32[3,256,512]{2,1,0:T(8,128)}) %all-reduce.10.cloned.1.call-update) | async-done | bytes 1572880 | tf_op jit(solution)/shard_map/psum | solution.py:13
  972.3 6.0 negate_bitcast_fusion
  (206 shorter events, 165.3 us)
Async XLA Ops:
  9.8 16.6 %all-to-all-start = ((s32[16,2,1]{1,2,0:T(1,128)}), s32[16,2,1]{1,2,0:T(1,128)S(1)}, u32[]{:S(2)}, u32[]{:S(2)}) async-start(s32[16,2,1]{1,2,0:T(1,128)} %bitcast.7), calls=%async_computation | async-start | bytes 16384 | tf_op jit(solution)/shard_map/all_to_all | solution.py:79
  26.4 59.1 %copy-start.16 = (bf16[1,3,1,256,3,1,256]{6,3,5,4,2,1,0:T(8,128)(2,1)S(1)}, bf16[1,3,1,256,3,1,256]{6,3,5,4,2,1,0:T(8,128)(2,1)}, u32[]{:S(2)}) copy-start(bf16[1,3,1,256,3,1,256]{6,3,5,4,2,1,0:T(8,128)(2,1)} %param.25) | copy-start | bytes 3538948
  26.4 59.1 %all-to-all-start.1 = ((bf16[32,256,256]{2,1,0:T(8,128)(2,1)}), bf16[32,256,256]{2,1,0:T(8,128)(2,1)}, u32[]{:S(2)}, u32[]{:S(2)}) async-start(bf16[32,256,256]{2,1,0:T(8,128)(2,1)} %broadcast_select_fusion), calls=%async_computation.1 | async-start | bytes 8388608 | tf_op jit(solution)/shard_map/all_to_all | solution.py:78
  33.8 146.5 %all-reduce.14.cloned.1.call-start = ((), (), s32[]{:S(2)}) async-start(), calls=%async_computation.7 | async-start | bytes 3145728 | tf_op jit(solution)/shard_map/psum | solution.py:13
  91.1 2.2 copy-start.3
  93.3 160.9 %all-gather.3.cloned.1.call-start = ((), (), s32[]{:S(2)}) async-start(), calls=%async_computation.2 | async-start | bytes 4718592 | tf_op jit(solution)/shard_map/all_gather | solution.py:139
  180.3 1.4 copy-start.11
  181.8 1.2 copy-start.5
  183.9 332.9 %all-reduce.8.cloned.1.call-start = ((), (), s32[]{:S(2)}) async-start(), calls=%async_computation.3 | async-start | bytes 3145728 | tf_op jit(solution)/shard_map/psum | solution.py:13
  260.6 1.0 copy-start.10
  422.1 2.1 copy-start.1
  422.2 196.8 %all-reduce.12.cloned.1.call-start = ((), (), s32[]{:S(2)}) async-start(), calls=%async_computation.6 | async-start | bytes 3145728 | tf_op jit(solution)/shard_map/psum | solution.py:13
  424.2 18.7 %copy-start.8 = (f32[3,256,256]{2,1,0:T(8,128)S(1)}, f32[3,256,256]{2,1,0:T(8,128)}, u32[]{:S(2)}) copy-start(f32[3,256,256]{2,1,0:T(8,128)} %get-tuple-element.105) | copy-start | bytes 2359300
  533.1 159.8 %all-gather.5.cloned.1.call-start = ((), (), s32[]{:S(2)}) async-start(), calls=%async_computation.4 | async-start | bytes 4718592 | tf_op jit(solution)/shard_map/all_gather | solution.py:139
  618.9 1.4 copy-start.12
  620.4 1.2 copy-start.6
  622.5 346.6 %all-reduce.10.cloned.1.call-start = ((), (), s32[]{:S(2)}) async-start(), calls=%async_computation.5 | async-start | bytes 3145728 | tf_op jit(solution)/shard_map/psum | solution.py:13
  695.8 1.2 copy-start.4
  703.9 1.0 copy-start.9
  729.7 0.7 copy-start.13
  853.7 4.0 copy-start.7
  865.4 3.1 copy-start.2
  868.5 1.8 copy-start.14
  868.5 1.8 copy-start.15
  875.4 1.6 copy-start
Sparse Core Ops, SparseCore 0:
  93.5 86.7 all-reduce.13
  184.0 70.1 all-gather.2
  422.3 94.4 all-reduce.7
  533.2 85.7 all-reduce.11
  622.6 70.1 all-gather.4
  874.7 94.3 all-reduce.9
